TPU v7x, 256 devices: a whole 4x4x8 slice. The times are simulated.
256 devices in a mesh: leaf: 32 (over x, y, core), mp: 8 (over z).
Axes of the slice: x: 4, y: 4, z: 8, core: 2. Of those that a mesh axis runs over, the one named last changes fastest.
Arguments:
- activations: bfloat16 [8192, 4096], P('leaf', 'mp'), may hold values from -6 to 6
- w_query: bfloat16 [4096, 2048], P(None, 'mp'), may hold values from -0.0625 to 0.0625
- w_key: bfloat16 [4096, 2048], P(None, 'mp'), may hold values from -0.0625 to 0.0625
- w_value: bfloat16 [4096, 2048], P(None, 'mp'), may hold values from -0.09375 to 0.09375
- w_out: bfloat16 [2048, 4096], P('mp'), may hold values from -0.70710678 to 0.70710678
- norm_gain: float32 [4096], P('mp'), may hold values from 0.1 to 1.9
- key_cache: bfloat16 [256, 256, 2048], P('leaf', None, 'mp'), may hold values from -6 to 6
- value_cache: bfloat16 [256, 256, 2048], P('leaf', None, 'mp'), may hold values from -6 to 6
- parent: int32 [256], replicated, may hold values from 0 to 255, as said below
- node_len: int32 [256], replicated, may hold values from 1 to 256, as said below
- req_leaf: int32 [128], replicated, may hold values from 0 to 255, as said below
Outputs:
- layer_out: bfloat16 [8192, 4096], P('leaf', 'mp')
Inputs may be any that keep to these rules, and one draw needn't show every extreme that they name: Exactly 4 nodes are their own parent (the roots); node n's cache is held by leaf index n // 8. Every request's leaf, its parent and that parent's parent are three distinct nodes, the last a root; no request's middle or leaf node is held by a leaf index that holds a root. `node_len`: every root has 256 live rows. `req_leaf`: over the 4 requests of one leaf index, the nodes of their paths counted with repetition lie at most 2 on any one holder, and their middle and leaf nodes at most 2; both bounds are reached on some holder for every leaf index.
All inputs are finite; a program needn't handle non-finite values.
Results may differ from a plain program's by a relative error of at most 0.03.
Values may be sent and summed in bfloat16 or wider, within the bound.
A program may use at most 128 MiB of HBM per device.

v0:
```python
import math
import jax
import jax.numpy as jnp
from jax import lax
from jax.sharding import PartitionSpec as P

D = 4096
HD = 128
TENANTS = 4
NODE_DEV = 8
REQ_LEN = 64
REQ_DEV = 4
rope_base = 500000.0
mask_value = -1e30
norm_eps = 1e-06


def rotate(values, positions):
    half_width = values.shape[-1] // 2
    inverse_freq = jnp.exp(
        jnp.arange(half_width, dtype=jnp.float32) * (-2.0 * math.log(rope_base) / values.shape[-1])
    )
    angles = positions.astype(jnp.float32)[:, None] * inverse_freq[None, :]
    cosine = jnp.cos(angles)[:, None, :]
    sine_part = jnp.sin(angles)[:, None, :]
    front_half = values[..., :half_width]
    back_half = values[..., half_width:]
    return jnp.concatenate(
        [front_half * cosine - back_half * sine_part, back_half * cosine + front_half * sine_part],
        axis=-1,
    )


def route_table(sender_nodes, leaf_count, capacity):
    holders = sender_nodes // NODE_DEV
    item_count = sender_nodes.shape[0]
    earlier = jnp.arange(item_count)[:, None] > jnp.arange(item_count)[None, :]
    same_holder = holders[:, None] == holders[None, :]
    ranks = jnp.sum(earlier & same_holder, axis=1)
    slot_table = (
        jnp.full((leaf_count, capacity), -1, jnp.int32).at[holders, ranks].set(sender_nodes)
    )
    return (holders, ranks, slot_table)


def node_attention(queries, keys, values, lengths, heads_local):
    blocks, row_total, width = queries.shape
    head_dim = width // heads_local
    query_heads = queries.reshape(blocks, row_total, heads_local, head_dim)
    key_heads = keys.reshape(blocks, keys.shape[1], heads_local, head_dim)
    value_heads = values.reshape(blocks, values.shape[1], heads_local, head_dim)
    scores = jnp.einsum(
        "nqhd,nkhd->nhqk", query_heads, key_heads, preferred_element_type=jnp.float32
    ) * head_dim ** (-0.5)
    live_mask = jnp.arange(keys.shape[1])[None, :] < lengths[:, None]
    scores = jnp.where(live_mask[:, None, None, :], scores, mask_value)
    highest = jnp.max(scores, axis=-1)
    weights = jnp.exp(scores - highest[..., None])
    totals = jnp.sum(weights, axis=-1)
    mixture = jnp.einsum(
        "nhqk,nkhd->nqhd",
        weights.astype(jnp.bfloat16),
        value_heads,
        preferred_element_type=jnp.float32,
    )
    result = (
        (mixture / jnp.transpose(totals, (0, 2, 1))[..., None])
        .astype(jnp.bfloat16)
        .reshape(blocks, row_total, width)
    )
    return (result, jnp.transpose(highest + jnp.log(totals), (0, 2, 1)))


def self_attention(queries, keys, values):
    head_dim = queries.shape[-1]
    row_total = queries.shape[1]
    scores = jnp.einsum(
        "rqhd,rkhd->rhqk", queries, keys, preferred_element_type=jnp.float32
    ) * head_dim ** (-0.5)
    causal = jnp.arange(row_total)[:, None] >= jnp.arange(row_total)[None, :]
    scores = jnp.where(causal[None, None], scores, mask_value)
    highest = jnp.max(scores, axis=-1)
    weights = jnp.exp(scores - highest[..., None])
    totals = jnp.sum(weights, axis=-1)
    mixture = jnp.einsum(
        "rhqk,rkhd->rqhd", weights.astype(jnp.bfloat16), values, preferred_element_type=jnp.float32
    )
    return (
        mixture / jnp.transpose(totals, (0, 2, 1))[..., None],
        jnp.transpose(highest + jnp.log(totals), (0, 2, 1)),
    )


def on_device(
    activations,
    w_query,
    w_key,
    w_value,
    w_out,
    norm_gain,
    key_cache,
    value_cache,
    parent,
    node_len,
    req_leaf,
):
    leaf_count = lax.axis_size("leaf")
    device = lax.axis_index("leaf")
    tok_rows = activations.shape[0]
    width_local = w_query.shape[1]
    heads_local = width_local // HD
    spread = leaf_count - TENANTS
    node_slots = 2 * ((REQ_DEV + spread - 1) // spread)
    all_slots = max(REQ_DEV // TENANTS, node_slots)
    columns = lax.all_gather(activations, "mp", axis=1, tiled=True)
    query_f, key_f, value_f = tuple(
        (
            jnp.dot(columns, matrix, preferred_element_type=jnp.float32)
            for matrix in (w_query, w_key, w_value)
        )
    )
    middle_all = parent[req_leaf]
    root_all = parent[middle_all]
    prefix = node_len[root_all] + node_len[middle_all] + node_len[req_leaf]
    mine_prefix = lax.dynamic_slice_in_dim(prefix, device * REQ_DEV, REQ_DEV)
    position = (mine_prefix[:, None] + jnp.arange(REQ_LEN, dtype=jnp.int32)[None, :]).reshape(
        tok_rows
    )
    queries = rotate(query_f.reshape(tok_rows, heads_local, HD), position).astype(jnp.bfloat16)
    keys = rotate(key_f.reshape(tok_rows, heads_local, HD), position).astype(jnp.bfloat16)
    values = value_f.astype(jnp.bfloat16)
    q_blocks = queries.reshape(REQ_DEV, REQ_LEN, width_local)
    self_out, self_lse = self_attention(
        queries.reshape(REQ_DEV, REQ_LEN, heads_local, HD),
        keys.reshape(REQ_DEV, REQ_LEN, heads_local, HD),
        values.reshape(REQ_DEV, REQ_LEN, heads_local, HD),
    )
    levels_all = jnp.stack([root_all, middle_all, req_leaf], axis=0).reshape(3, leaf_count, REQ_DEV)
    level_count = levels_all.shape[0]
    per_sender = jnp.transpose(levels_all, (1, 0, 2)).reshape(leaf_count, level_count * REQ_DEV)
    holders_all, ranks_all, tables = jax.vmap(
        lambda sender_nodes: route_table(sender_nodes, leaf_count, all_slots)
    )(per_sender)
    my_holder = holders_all[device]
    my_rank = ranks_all[device]
    item_request = jnp.arange(level_count * REQ_DEV) % REQ_DEV
    outgoing = (
        jnp.zeros((leaf_count, all_slots, REQ_LEN, width_local), jnp.bfloat16)
        .at[my_holder, my_rank]
        .set(q_blocks[item_request])
    )
    arrived = lax.all_to_all(outgoing, "leaf", split_axis=0, concat_axis=0, tiled=True)
    slot_nodes = tables[:, device].reshape(-1)
    filled = slot_nodes >= 0
    local_slot = jnp.where(filled, slot_nodes - device * NODE_DEV, 0)
    lengths = jnp.where(filled, node_len[jnp.maximum(slot_nodes, 0)], 0)
    node_out, node_lse = node_attention(
        arrived.reshape(leaf_count * all_slots, REQ_LEN, width_local),
        key_cache[local_slot],
        value_cache[local_slot],
        lengths,
        heads_local,
    )
    back_out = lax.all_to_all(
        node_out.reshape(leaf_count, all_slots, REQ_LEN, width_local),
        "leaf",
        split_axis=0,
        concat_axis=0,
        tiled=True,
    )
    back_lse = lax.all_to_all(
        node_lse.reshape(leaf_count, all_slots, REQ_LEN, heads_local).astype(jnp.bfloat16),
        "leaf",
        split_axis=0,
        concat_axis=0,
        tiled=True,
    ).astype(jnp.float32)
    got_out = back_out[my_holder, my_rank].reshape(level_count, REQ_DEV, REQ_LEN, width_local)
    got_lse = back_lse[my_holder, my_rank].reshape(level_count, REQ_DEV, REQ_LEN, heads_local)
    partial_out = jnp.concatenate(
        [got_out.reshape(3, REQ_DEV, REQ_LEN, heads_local, HD).astype(jnp.float32), self_out[None]],
        axis=0,
    )
    partial_lse = jnp.concatenate([got_lse, self_lse[None]], axis=0)
    highest = jnp.max(partial_lse, axis=0)
    factor = jnp.exp(partial_lse - highest[None])
    merged = jnp.sum(factor[..., None] * partial_out, axis=0) / jnp.sum(factor, axis=0)[..., None]
    attn = merged.astype(jnp.bfloat16).reshape(tok_rows, width_local)
    partial_value = jnp.dot(attn, w_out, preferred_element_type=jnp.float32)
    projected = lax.psum_scatter(
        partial_value.astype(jnp.bfloat16), "mp", scatter_dimension=1, tiled=True
    ).astype(jnp.float32)
    squares = lax.psum(jnp.sum(projected * projected, axis=1), "mp")
    row_scale = lax.rsqrt(squares / D + norm_eps)
    return (
        activations.astype(jnp.float32) + norm_gain[None, :] * projected * row_scale[:, None]
    ).astype(jnp.bfloat16)


def solution(mesh):
    in_specs = (
        P("leaf", "mp"),
        P(None, "mp"),
        P(None, "mp"),
        P(None, "mp"),
        P("mp", None),
        P("mp"),
        P("leaf", None, "mp"),
        P("leaf", None, "mp"),
        P(),
        P(),
        P(),
    )
    out_specs = P("leaf", "mp")
    return jax.shard_map(
        on_device, mesh=mesh, in_specs=in_specs, out_specs=out_specs, check_vma=False
    )
```

profile of v0, /device:TPU:4, one launch (start us, length us, event | category | flops | bytes accessed | tf_op | source)
XLA Modules:
  0.0 255.1 jit_solution(10342015116051803166)
XLA Ops:
  6.5 0.7 all-gather.2.cloned.1.call-update
  7.3 0.7 compare_select_fusion.8
  7.9 1.6 gather_fusion.5
  9.6 1.6 gather_fusion
  11.2 1.6 gather_fusion.1
  12.9 1.6 gather_fusion.4
  14.5 0.7 stack.14
  15.5 1.6 gather_fusion.3
  18.2 0.3 multiply_cosine_fusion
  18.5 34.5 %all-gather.2.cloned.1.call-done = bf16[256,4096]{1,0:T(8,128)(2,1)} async-done(((bf16[256,512]{1,0:T(8,128)(2,1)}), bf16[256,4096]{1,0:T(8,128)(2,1)}) %all-gather.2.cloned.1.call-update) | async-done | bytes 2097168 | tf_op jit(solution)/shard_map/all_gather | solution.py:115
  53.0 3.3 %fusion.69 = f32[256,256]{0,1:T(8,128)S(1)} fusion(bf16[256,4096]{1,0:T(8,128)(2,1)} %all-gather.2.cloned.1.call-done, bf16[4096,256]{1,0:T(8,128)(2,1)} %param.13), kind=kOutput, calls=%fused_computation.148 | convolution fusion | flops 536870912 | bytes 4456448 | tf_op jit(solution)/shard_map/dot_general | solution.py:118
  56.4 1.0 fusion.68
  57.7 0.6 gather_fusion.6
  58.3 1.6 broadcast_in_dim.33
  59.9 2.5 scatter_fusion
  62.4 7.5 %all-to-all-start = ((bf16[32,2,64,256]{3,2,1,0:T(8,128)(2,1)}), bf16[32,2,64,256]{3,2,1,0:T(8,128)(2,1)}, u32[]{:S(2)}, u32[]{:S(2)}) async-start(bf16[32,2,64,256]{3,2,1,0:T(8,128)(2,1)} %scatter_fusion), calls=%async_computation | async-start | bytes 4194304 | tf_op jit(solution)/shard_map/all_to_all | solution.py:152
  70.4 24.3 %scatter_fusion.1 = s32[32,32,2]{1,0,2:T(8,128)S(1)} fusion(s32[32,32,2]{1,0,2:T(8,128)S(1)} %broadcast_in_dim.30, s32[384]{0:T(512)S(1)} %reshape.587, s32[384]{0:T(512)S(1)} %reshape.589), kind=kCustom, calls=%fused_computation.12 | custom fusion | bytes 9216 | tf_op jit(solution)/shard_map/vmap()/scatter | solution.py:41
  94.9 0.3 copy.152
  95.3 0.3 copy.153
  95.7 0.8 gather_fusion.2
  96.5 0.3 copy.155
  97.0 5.3 %gather_fusion.7 = bf16[64,256,256]{2,1,0:T(8,128)(2,1)} fusion(bf16[8,256,256]{2,1,0:T(8,128)(2,1)S(1)} %copy-done.2, s32[1024]{0:T(1024)S(1)} %pad_clamp_fusion), kind=kCustom, calls=%fused_computation.7 | custom fusion | bytes 16777472 | tf_op jit(solution)/shard_map/gather | solution.py:159
  102.3 6.5 %gather_fusion.9 = bf16[64,256,256]{2,1,0:T(8,128)(2,1)} fusion(bf16[8,256,256]{2,1,0:T(8,128)(2,1)} %param.18, s32[1024]{0:T(1024)S(1)} %pad_clamp_fusion), kind=kCustom, calls=%fused_computation.9 | custom fusion | bytes 16777472 | tf_op jit(solution)/shard_map/gather | solution.py:160
  108.9 4.0 %reshape_reshape.7 = bf16[64,64,2,128]{3,2,1,0:T(2,128)(2,1)} reshape(bf16[32,2,64,256]{3,2,1,0:T(8,128)(2,1)} %all-to-all-done) | data formatting | bytes 4194304 | tf_op jit(solution)/shard_map/reshape;reshape | solution.py:49
  112.9 7.2 %fusion.6 = (f32[64,2,64]{2,1,0:T(2,128)S(1)}, f32[64,2,64,256]{3,2,1,0:T(8,128)S(1)}) fusion(pred[64,256]{1,0:T(8,128)(4,1)S(1)} %iota_compare_fusion, bf16[64,64,2,128]{3,2,1,0:T(2,128)(2,1)} %reshape_reshape.7, bf16[64,256,256]{2,1,0:T(8,128)(2,1)} %gather_fusion.7), kind=kOutput, calls=%fused_computation.21 | convolution fusion | flops 543154176 | bytes 18923520 | tf_op jit(solution)/shard_map/nqhd,nkhd->nhqk/dot_general | solution.py:52
  120.1 3.6 %fusion.8 = f32[64,2,64]{2,1,0:T(2,128)S(1)} fusion(f32[64,2,64,256]{3,2,1,0:T(8,128)S(1)} %get-tuple-element.25, f32[64,2,64]{2,1,0:T(2,128)S(1)} %get-tuple-element.24, pred[64,256]{1,0:T(8,128)(4,1)S(1)} %iota_compare_fusion), kind=kLoop, calls=%fused_computation.23 | loop fusion | flops 8380416 | bytes 8470528 | tf_op jit(solution)/shard_map/reduce_sum | solution.py:59
  123.7 0.7 reshape.599
  124.4 7.4 %all-to-all-start.1 = ((bf16[32,2,128]{2,1,0:T(2,128)(2,1)}), bf16[32,2,128]{2,1,0:T(2,128)(2,1)S(1)}, u32[]{:S(2)}, u32[]{:S(2)}) async-start(bf16[32,2,128]{2,1,0:T(2,128)(2,1)} %reshape.599), calls=%async_computation.1 | async-start | bytes 32768 | tf_op jit(solution)/shard_map/all_to_all | solution.py:171
  131.8 7.5 %fusion.10 = bf16[64,64,2,128]{3,1,2,0:T(8,128)(2,1)S(1)} fusion(f32[64,64,2]{1,2,0:T(2,128)S(1)} %bitcast.135, f32[64,2,64,256]{3,2,1,0:T(8,128)} %copy-done.3, f32[64,2,64]{2,1,0:T(2,128)S(1)} %get-tuple-element.24, pred[64,256]{1,0:T(8,128)(4,1)S(1)} %iota_compare_fusion, bf16[64,256,256]{2,1,0:T(8,128)(2,1)} %gather_fusion.9), kind=kOutput, calls=%fused_computation.26 | convolution fusion | flops 547356672 | bytes 18956288 | tf_op jit(solution)/shard_map/nhqk,nkhd->nqhd/dot_general | solution.py:60
  139.4 3.5 %copy.167 = bf16[64,64,2,128]{3,2,1,0:T(2,128)(2,1)} copy(bf16[64,64,2,128]{3,1,2,0:T(8,128)(2,1)S(1)} %fusion.10) | data formatting | bytes 4194304 | tf_op jit(solution)/shard_map/convert_element_type | solution.py:68
  142.9 4.4 %reshape_reshape.8 = bf16[32,2,64,256]{3,2,1,0:T(8,128)(2,1)} reshape(bf16[64,64,2,128]{3,2,1,0:T(2,128)(2,1)} %copy.167) | data formatting | bytes 4194304 | tf_op jit(solution)/shard_map/reshape;reshape | solution.py:165
  147.3 7.4 %all-to-all-start.2 = ((bf16[32,2,64,256]{3,2,1,0:T(8,128)(2,1)}), bf16[32,2,64,256]{3,2,1,0:T(8,128)(2,1)}, u32[]{:S(2)}, u32[]{:S(2)}) async-start(bf16[32,2,64,256]{3,2,1,0:T(8,128)(2,1)} %reshape_reshape.8), calls=%async_computation.2 | async-start | bytes 4194304 | tf_op jit(solution)/shard_map/all_to_all | solution.py:164
  155.9 2.9 %convolution_convert_fusion.1 = bf16[256,256]{1,0:T(8,128)(2,1)S(1)} fusion(bf16[256,4096]{1,0:T(8,128)(2,1)} %all-gather.2.cloned.1.call-done, bf16[4096,256]{1,0:T(8,128)(2,1)} %param.14), kind=kOutput, calls=%fused_computation.37 | convolution fusion | flops 536936448 | bytes 4325376 | tf_op jit(solution)/shard_map/dot_general | solution.py:118
  158.9 0.3 fusion.67
  159.2 0.2 fusion.18
  159.5 0.9 copy.170
  160.5 0.7 gather_fusion.8
  161.2 0.2 copy.165
  161.6 19.1 %all-to-all-done.2 = bf16[32,2,64,256]{3,2,1,0:T(8,128)(2,1)} async-done(((bf16[32,2,64,256]{3,2,1,0:T(8,128)(2,1)}), bf16[32,2,64,256]{3,2,1,0:T(8,128)(2,1)}, u32[]{:S(2)}, u32[]{:S(2)}) %all-to-all-start.2) | async-done | bytes 2097184 | tf_op jit(solution)/shard_map/all_to_all | solution.py:164
  180.7 3.0 %gather_fusion.10 = bf16[12,64,256]{2,1,0:T(8,128)(2,1)} fusion(bf16[32,2,64,256]{3,2,1,0:T(8,128)(2,1)} %all-to-all-done.2, s32[12]{0:T(128)S(1)} %get-tuple-element.20), kind=kCustom, calls=%fused_computation.10 | custom fusion | bytes 786528 | tf_op jit(solution)/shard_map/gather | solution.py:178
  183.7 1.4 reshape.496
  185.1 2.3 fusion.23
  187.4 0.3 divide_convert_fusion
  187.7 2.1 convolution_convert_fusion
  189.8 40.3 %reduce-scatter.2.cloned.1.call-done = bf16[256,512]{1,0:T(8,128)(2,1)} async-done(((bf16[256,4096]{1,0:T(8,128)(2,1)}), bf16[256,512]{1,0:T(8,128)(2,1)}) %reduce-scatter.2.cloned.1.call-update) | async-done | bytes 262160 | tf_op jit(solution)/shard_map/reduce_scatter | solution.py:190
  230.1 1.1 fusion.27
  231.2 15.3 %psum.7 = f32[256]{0:T(256)S(1)} all-reduce(f32[256]{0:T(256)S(1)} %fusion.27), channel_id=1, replica_groups=mesh['leaf'=32,'mp'=8] {'mp'}, use_global_device_ids=true, to_apply=%region_12.13 | all-reduce | flops 256 | bytes 2048 | tf_op jit(solution)/shard_map/psum | solution.py:193
  246.5 1.8 fusion.26
  (87 shorter events, 4.3 us)
Async XLA Ops:
  6.5 181.2 %copy-start = (bf16[256,4096]{1,0:T(8,128)(2,1)S(1)}, bf16[256,4096]{1,0:T(8,128)(2,1)}, u32[]{:S(2)}) copy-start(bf16[256,4096]{1,0:T(8,128)(2,1)} %param.15) | copy-start | bytes 6291460
  6.5 46.4 %all-gather.2.cloned.1.call-start = ((), (), s32[]{:S(2)}) async-start(), calls=%async_computation.4 | async-start | bytes 2359296 | tf_op jit(solution)/shard_map/all_gather | solution.py:115
  53.0 3.3 %copy-start.4 = (bf16[256,4096]{1,0:T(8,128)(2,1)S(1)}, bf16[256,4096]{1,0:T(8,128)(2,1)}, u32[]{:S(2)}) copy-start(bf16[256,4096]{1,0:T(8,128)(2,1)} %all-gather.2.cloned.1.call-done) | copy-start | bytes 6291460
  53.0 3.5 %copy-start.5 = (bf16[4096,256]{1,0:T(8,128)(2,1)S(1)}, bf16[4096,256]{1,0:T(8,128)(2,1)}, u32[]{:S(2)}) copy-start(bf16[4096,256]{1,0:T(8,128)(2,1)} %param.12) | copy-start | bytes 6291460
  62.4 46.5 %all-to-all-start = ((bf16[32,2,64,256]{3,2,1,0:T(8,128)(2,1)}), bf16[32,2,64,256]{3,2,1,0:T(8,128)(2,1)}, u32[]{:S(2)}, u32[]{:S(2)}) async-start(bf16[32,2,64,256]{3,2,1,0:T(8,128)(2,1)} %scatter_fusion), calls=%async_computation | async-start | bytes 4194304 | tf_op jit(solution)/shard_map/all_to_all | solution.py:152
  70.4 25.3 %copy-start.1 = (s32[256]{0:T(256)S(1)}, s32[256]{0:T(256)}, u32[]{:S(2)}) copy-start(s32[256]{0:T(256)} %param.20) | copy-start | bytes 3076
  70.4 26.6 %copy-start.2 = (bf16[8,256,256]{2,1,0:T(8,128)(2,1)S(1)}, bf16[8,256,256]{2,1,0:T(8,128)(2,1)}, u32[]{:S(2)}) copy-start(bf16[8,256,256]{2,1,0:T(8,128)(2,1)} %param.17) | copy-start | bytes 3145732
  120.1 3.6 %copy-start.3 = (f32[64,2,64,256]{3,2,1,0:T(8,128)}, f32[64,2,64,256]{3,2,1,0:T(8,128)S(1)}, u32[]{:S(2)}) copy-start(f32[64,2,64,256]{3,2,1,0:T(8,128)S(1)} %get-tuple-element.25) | copy-start | bytes 25165828
  124.4 22.8 %all-to-all-start.1 = ((bf16[32,2,128]{2,1,0:T(2,128)(2,1)}), bf16[32,2,128]{2,1,0:T(2,128)(2,1)S(1)}, u32[]{:S(2)}, u32[]{:S(2)}) async-start(bf16[32,2,128]{2,1,0:T(2,128)(2,1)} %reshape.599), calls=%async_computation.1 | async-start | bytes 32768 | tf_op jit(solution)/shard_map/all_to_all | solution.py:171
  147.3 33.4 %all-to-all-start.2 = ((bf16[32,2,64,256]{3,2,1,0:T(8,128)(2,1)}), bf16[32,2,64,256]{3,2,1,0:T(8,128)(2,1)}, u32[]{:S(2)}, u32[]{:S(2)}) async-start(bf16[32,2,64,256]{3,2,1,0:T(8,128)(2,1)} %reshape_reshape.8), calls=%async_computation.2 | async-start | bytes 4194304 | tf_op jit(solution)/shard_map/all_to_all | solution.py:164
  154.7 75.4 %reduce-scatter.2.cloned.1.call-start = ((), (), s32[]{:S(2)}) async-start(), calls=%async_computation.5 | async-start | bytes 2359296 | tf_op jit(solution)/shard_map/reduce_scatter | solution.py:190
  185.0 61.5 %copy-start.7 = (f32[512]{0:T(512)S(1)}, f32[512]{0:T(512)}, u32[]{:S(2)}) copy-start(f32[512]{0:T(512)} %param.16) | copy-start | bytes 6148
  187.4 59.1 %copy-start.6 = (bf16[256,512]{1,0:T(8,128)(2,1)S(1)}, bf16[256,512]{1,0:T(8,128)(2,1)}, u32[]{:S(2)}) copy-start(bf16[256,512]{1,0:T(8,128)(2,1)} %param.11) | copy-start | bytes 786436
Sparse Core Ops, SparseCore 0:
  9.1 43.7 all-gather.1
  189.9 40.1 reduce-scatter.1
where the time goes:
time: 256 us; the launch traced here: 255 us
  waiting for transfers between devices  94.6 us (37%)
  local copies, waits for them, and re-layouts  73.6 us (29%)
  matrix products  24.5 us (10%)
  starting transfers between devices  22.4 us (9%)
  blocking collectives  15.3 us (6%)
  between operations  13.9 us (5%)
  other arithmetic  10.8 us (4%)
    reduce_scatter x1, waiting for transfers between devices, on_device(): lax.psum_scatter(partial_value.astype(jnp.bfloat16), 'mp', scatter_dimens...  40.3 us
    all_gather x1, waiting for transfers between devices, on_device(): columns = lax.all_gather(activations, 'mp', axis=1, tiled=True)  34.5 us
    scatter x3, local copies, waits for them, and re-layouts, route_table(): jnp.full((leaf_count, capacity), -1, jnp.int32).at[holders, ranks]  24.5 us
    all_to_all x1, waiting for transfers between devices, on_device(): lax.all_to_all(node_out.reshape(leaf_count, all_slots, REQ_LEN, width_loc...  19.1 us
    psum x1, blocking collectives, on_device(): squares = lax.psum(jnp.sum(projected * projected, axis=1), 'mp')  15.3 us
    dot_general x1, matrix products, node_attention(): jnp.einsum('nhqk,nkhd->nqhd', weights.astype(jnp.bfloat16), value_heads,...  7.53 us
    all_to_all x1, starting transfers between devices, on_device(): lax.all_to_all(outgoing, 'leaf', split_axis=0, concat_axis=0, tiled=True)  7.5 us
    all_to_all x1, starting transfers between devices, on_device(): lax.all_to_all(node_out.reshape(leaf_count, all_slots, REQ_LEN, width_loc...  7.43 us
  transfers between devices with their start and end apart: 5, of which 3 were waited for; matrix products, arithmetic and copies ran while one was open for 28% of the time, Pallas kernels for 0%

commit v1 on v0

--- a/solution.py
+++ b/solution.py
@@ -13,6 +13,26 @@
 rope_base = 500000.0
 mask_value = -1e30
 norm_eps = 1e-06
+
+
+def run_the_record(x_local, along_axis, at_axis=1):
+    pool = []
+    ndev = jax.lax.psum(1, axis_name=along_axis)
+    for d in range(ndev):
+        pool.append((d, (d + 1) % ndev))
+    panels = []
+    for d in range(ndev):
+        panels.append((d, (d - 1) % ndev))
+    part_next, piece_next = ([x_local], [x_local])
+    for _ in range(ndev // 2):
+        ready = jax.lax.ppermute(part_next[-1], axis_name=along_axis, perm=pool)
+        part_next.append(ready)
+    for _ in range((ndev - 1) // 2):
+        after = jax.lax.ppermute(piece_next[-1], along_axis, panels)
+        piece_next.append(after)
+    carry_out = jnp.concatenate([*part_next[::-1], *piece_next[1:]], axis=at_axis)
+    state_now = jax.lax.axis_index(along_axis)
+    return jnp.roll(carry_out, (state_now - ndev // 2) * x_local.shape[at_axis], axis=at_axis)
 
 
 def rotate(values, positions):
@@ -112,7 +132,7 @@
     spread = leaf_count - TENANTS
     node_slots = 2 * ((REQ_DEV + spread - 1) // spread)
     all_slots = max(REQ_DEV // TENANTS, node_slots)
-    columns = lax.all_gather(activations, "mp", axis=1, tiled=True)
+    columns = run_the_record(activations, "mp")
     query_f, key_f, value_f = tuple(
         (
             jnp.dot(columns, matrix, preferred_element_type=jnp.float32)

time: 256 us -> 270 us (1.055)
  starting transfers between devices: 22.4 us -> 34.6 us
  local copies, waits for them, and re-layouts: 73.6 us -> 83.8 us
  waiting for transfers between devices: 94.6 us -> 86.7 us
    all_gather x1 -> x0, waiting for transfers between devices: 34.5 us -> none  [on_device(): columns = lax.all_gather(activations, 'mp', axis=1, tiled=True)]
    ppermute x0 -> x7, waiting for transfers between devices: none -> 17.4 us  [the longest x4 17.4 us: run_the_record(): ready = jax.lax.ppermute(part_next[-1], axis_name=along_axis, perm=pool)]
    ppermute x0 -> x7, starting transfers between devices: none -> 12.6 us  [the longest x3 10.6 us: run_the_record(): after = jax.lax.ppermute(piece_next[-1], along_axis, panels)]
    all_to_all x1, waiting for transfers between devices: 0.01 us -> 9.08 us  [on_device(): lax.all_to_all(outgoing, 'leaf', split_axis=0, concat_axis=0, tiled=True)]
    unnamed x18 -> x41, local copies, waits for them, and re-layouts: 0.98 us -> 7.04 us
  transfers between devices with their start and end apart: 5 -> 11, of which waited for: 3 -> 6; matrix products, arithmetic and copies ran while one was open for 28% -> 29% of each run, Pallas kernels for 0% -> 0%
where the time goes in v1:
time: 270 us; the launch traced here: 269 us
  waiting for transfers between devices  86.7 us (32%)
  local copies, waits for them, and re-layouts  83.8 us (31%)
  starting transfers between devices  34.6 us (13%)
  matrix products  22.2 us (8%)
  blocking collectives  15.2 us (6%)
  between operations  14.2 us (5%)
  other arithmetic  12.1 us (4%)
    reduce_scatter x1, waiting for transfers between devices, on_device(): lax.psum_scatter(partial_value.astype(jnp.bfloat16), 'mp', scatter_dimens...  41.3 us
    scatter x3, local copies, waits for them, and re-layouts, route_table(): jnp.full((leaf_count, capacity), -1, jnp.int32).at[holders, ranks]  24.5 us
    all_to_all x1, waiting for transfers between devices, on_device(): lax.all_to_all(node_out.reshape(leaf_count, all_slots, REQ_LEN, width_loc...  19 us
    ppermute x4, waiting for transfers between devices, run_the_record(): ready = jax.lax.ppermute(part_next[-1], axis_name=along_axis, perm=pool)  17.4 us
    psum x1, blocking collectives, on_device(): squares = lax.psum(jnp.sum(projected * projected, axis=1), 'mp')  15.2 us
    ppermute x3, starting transfers between devices, run_the_record(): after = jax.lax.ppermute(piece_next[-1], along_axis, panels)  10.6 us
    all_to_all x1, waiting for transfers between devices, on_device(): lax.all_to_all(outgoing, 'leaf', split_axis=0, concat_axis=0, tiled=True)  9.08 us
    all_to_all x1, starting transfers between devices, on_device(): lax.all_to_all(outgoing, 'leaf', split_axis=0, concat_axis=0, tiled=True)  7.67 us
  transfers between devices with their start and end apart: 11, of which 6 were waited for; matrix products, arithmetic and copies ran while one was open for 29% of the time, Pallas kernels for 0%

profile of v1, /device:TPU:4, one launch (start us, length us, event | category | flops | bytes accessed | tf_op | source)
XLA Modules:
  0.0 268.8 jit_solution(13134655070118880200)
XLA Ops:
  6.5 1.9 collective-permute-start
  8.5 3.9 %collective-permute-start.4 = (bf16[256,512]{1,0:T(8,128)(2,1)}, bf16[256,512]{1,0:T(8,128)(2,1)S(1)}, u32[]{:S(2)}, u32[]{:S(2)}) collective-permute-start(bf16[256,512]{1,0:T(8,128)(2,1)} %param.11), channel_id=1, source_target_pairs={{0,7},{1,0},{2,1},{3,2},{4,3},{5,4},{6,5},{7,6},{8,15},{9,8},{10,9... | collective-permute-start | bytes 786440 | tf_op jit(solution)/shard_map/ppermute | solution.py:31
  13.8 1.6 gather_fusion
  15.6 1.6 gather_fusion.1
  17.7 1.6 gather_fusion.5
  19.4 1.6 gather_fusion.4
  21.5 24.3 %scatter_fusion.1 = s32[32,32,2]{1,0,2:T(8,128)S(1)} fusion(s32[32,32,2]{1,0,2:T(8,128)S(1)} %broadcast_in_dim.30, s32[384]{0:T(512)S(1)} %reshape.587, s32[384]{0:T(512)S(1)} %reshape.589), kind=kCustom, calls=%fused_computation.12 | custom fusion | bytes 9216 | tf_op jit(solution)/shard_map/vmap()/scatter | solution.py:61
  47.0 1.3 gather_fusion.3
  48.8 8.6 %collective-permute-done.1 = bf16[256,512]{1,0:T(8,128)(2,1)S(1)} collective-permute-done((bf16[256,512]{1,0:T(8,128)(2,1)S(1)}, bf16[256,512]{1,0:T(8,128)(2,1)S(1)}, u32[]{:S(2)}, u32[]{:S(2)}) %collective-permute-start.1) | collective-permute-done | bytes 262176 | tf_op jit(solution)/shard_map/ppermute | solution.py:28
  57.5 3.2 %collective-permute-start.5 = (bf16[256,512]{1,0:T(8,128)(2,1)S(1)}, bf16[256,512]{1,0:T(8,128)(2,1)}, u32[]{:S(2)}, u32[]{:S(2)}) collective-permute-start(bf16[256,512]{1,0:T(8,128)(2,1)S(1)} %collective-permute-done.4), channel_id=1, source_target_pairs={{0,7},{1,0},{2,1},{3,2},{4,3},{5,4},{6,5},{7,6},{8,15},{9,8},{10,9... | collective-permute-start | bytes 786440 | tf_op jit(solution)/shard_map/ppermute | solution.py:31
  60.7 4.8 %collective-permute-done.2 = bf16[256,512]{1,0:T(8,128)(2,1)} collective-permute-done((bf16[256,512]{1,0:T(8,128)(2,1)S(1)}, bf16[256,512]{1,0:T(8,128)(2,1)}, u32[]{:S(2)}, u32[]{:S(2)}) %collective-permute-start.2) | collective-permute-done | bytes 262176 | tf_op jit(solution)/shard_map/ppermute | solution.py:28
  66.0 3.5 %collective-permute-start.6 = (bf16[256,512]{1,0:T(8,128)(2,1)}, bf16[256,512]{1,0:T(8,128)(2,1)S(1)}, u32[]{:S(2)}, u32[]{:S(2)}) collective-permute-start(bf16[256,512]{1,0:T(8,128)(2,1)} %collective-permute-done.5), channel_id=1, source_target_pairs={{0,7},{1,0},{2,1},{3,2},{4,3},{5,4},{6,5},{7,6},{8,15},{9,8},{10,9... | collective-permute-start | bytes 786440 | tf_op jit(solution)/shard_map/ppermute | solution.py:31
  69.5 4.0 %collective-permute-done.3 = bf16[256,512]{1,0:T(8,128)(2,1)} collective-permute-done((bf16[256,512]{1,0:T(8,128)(2,1)}, bf16[256,512]{1,0:T(8,128)(2,1)}, u32[]{:S(2)}, u32[]{:S(2)}) %collective-permute-start.3) | collective-permute-done | bytes 262176 | tf_op jit(solution)/shard_map/ppermute | solution.py:28
  73.5 1.0 constant_dynamic-update-slice_fusion.15
  74.5 1.0 constant_dynamic-update-slice_fusion.14
  75.6 1.0 constant_dynamic-update-slice_fusion.9
  76.6 1.0 constant_dynamic-update-slice_fusion.7
  77.6 1.1 constant_dynamic-update-slice_fusion.6
  78.8 1.0 constant_dynamic-update-slice_fusion.1
  80.9 1.0 fusion.20
  82.8 1.3 gather_fusion.6
  84.1 1.6 broadcast_in_dim.33
  85.7 2.8 %scatter_fusion = bf16[32,2,64,256]{3,2,1,0:T(8,128)(2,1)} fusion(bf16[32,2,64,256]{3,2,1,0:T(8,128)(2,1)} %broadcast_in_dim.33, s32[12]{0:T(128)S(1)} %get-tuple-element.21, bf16[12,64,256]{2,1,0:T(8,128)(2,1)} %gather_fusion.6), kind=kCustom, calls=%fused_computation.11 | custom fusion | bytes 1179744 | tf_op jit(solution)/shard_map/scatter | solution.py:170
  88.6 7.7 %all-to-all-start = ((bf16[32,2,64,256]{3,2,1,0:T(8,128)(2,1)}), bf16[32,2,64,256]{3,2,1,0:T(8,128)(2,1)}, u32[]{:S(2)}, u32[]{:S(2)}) async-start(bf16[32,2,64,256]{3,2,1,0:T(8,128)(2,1)} %scatter_fusion), calls=%async_computation | async-start | bytes 4194304 | tf_op jit(solution)/shard_map/all_to_all | solution.py:172
  96.2 1.0 copy.152
  98.7 1.6 copy.155
  101.2 5.3 %gather_fusion.7 = bf16[64,256,256]{2,1,0:T(8,128)(2,1)} fusion(bf16[8,256,256]{2,1,0:T(8,128)(2,1)S(1)} %copy-done.2, s32[1024]{0:T(1024)S(1)} %pad_clamp_fusion), kind=kCustom, calls=%fused_computation.7 | custom fusion | bytes 16777472 | tf_op jit(solution)/shard_map/gather | solution.py:179
  106.5 6.5 %gather_fusion.9 = bf16[64,256,256]{2,1,0:T(8,128)(2,1)} fusion(bf16[8,256,256]{2,1,0:T(8,128)(2,1)} %param.18, s32[1024]{0:T(1024)S(1)} %pad_clamp_fusion), kind=kCustom, calls=%fused_computation.9 | custom fusion | bytes 16777472 | tf_op jit(solution)/shard_map/gather | solution.py:180
  113.1 9.1 %all-to-all-done = bf16[32,2,64,256]{3,2,1,0:T(8,128)(2,1)} async-done(((bf16[32,2,64,256]{3,2,1,0:T(8,128)(2,1)}), bf16[32,2,64,256]{3,2,1,0:T(8,128)(2,1)}, u32[]{:S(2)}, u32[]{:S(2)}) %all-to-all-start) | async-done | bytes 2097184 | tf_op jit(solution)/shard_map/all_to_all | solution.py:172
  122.2 4.0 %reshape_reshape.7 = bf16[64,64,2,128]{3,2,1,0:T(2,128)(2,1)} reshape(bf16[32,2,64,256]{3,2,1,0:T(8,128)(2,1)} %all-to-all-done) | data formatting | bytes 4194304 | tf_op jit(solution)/shard_map/reshape;reshape | solution.py:69
  126.2 7.2 %fusion.6 = (f32[64,2,64]{2,1,0:T(2,128)S(1)}, f32[64,2,64,256]{3,2,1,0:T(8,128)S(1)}) fusion(pred[64,256]{1,0:T(8,128)(4,1)S(1)} %iota_compare_fusion, bf16[64,64,2,128]{3,2,1,0:T(2,128)(2,1)} %reshape_reshape.7, bf16[64,256,256]{2,1,0:T(8,128)(2,1)} %gather_fusion.7), kind=kOutput, calls=%fused_computation.21 | convolution fusion | flops 543154176 | bytes 18923520 | tf_op jit(solution)/shard_map/nqhd,nkhd->nhqk/dot_general | solution.py:72
  133.4 3.6 %fusion.8 = f32[64,2,64]{2,1,0:T(2,128)S(1)} fusion(f32[64,2,64,256]{3,2,1,0:T(8,128)S(1)} %get-tuple-element.25, f32[64,2,64]{2,1,0:T(2,128)S(1)} %get-tuple-element.24, pred[64,256]{1,0:T(8,128)(4,1)S(1)} %iota_compare_fusion), kind=kLoop, calls=%fused_computation.23 | loop fusion | flops 8380416 | bytes 8470528 | tf_op jit(solution)/shard_map/reduce_sum | solution.py:79
  137.7 6.8 %all-to-all-start.1 = ((bf16[32,2,128]{2,1,0:T(2,128)(2,1)}), bf16[32,2,128]{2,1,0:T(2,128)(2,1)S(1)}, u32[]{:S(2)}, u32[]{:S(2)}) async-start(bf16[32,2,128]{2,1,0:T(2,128)(2,1)} %reshape.599), calls=%async_computation.1 | async-start | bytes 32768 | tf_op jit(solution)/shard_map/all_to_all | solution.py:191
  144.6 7.5 %fusion.10 = bf16[64,64,2,128]{3,1,2,0:T(8,128)(2,1)S(1)} fusion(f32[64,64,2]{1,2,0:T(2,128)S(1)} %bitcast.132, f32[64,2,64,256]{3,2,1,0:T(8,128)} %copy-done.3, f32[64,2,64]{2,1,0:T(2,128)S(1)} %get-tuple-element.24, pred[64,256]{1,0:T(8,128)(4,1)S(1)} %iota_compare_fusion, bf16[64,256,256]{2,1,0:T(8,128)(2,1)} %gather_fusion.9), kind=kOutput, calls=%fused_computation.26 | convolution fusion | flops 547356672 | bytes 18956288 | tf_op jit(solution)/shard_map/nhqk,nkhd->nqhd/dot_general | solution.py:80
  152.1 3.5 %copy.167 = bf16[64,64,2,128]{3,2,1,0:T(2,128)(2,1)} copy(bf16[64,64,2,128]{3,1,2,0:T(8,128)(2,1)S(1)} %fusion.10) | data formatting | bytes 4194304 | tf_op jit(solution)/shard_map/convert_element_type | solution.py:88
  155.6 4.4 %reshape_reshape.8 = bf16[32,2,64,256]{3,2,1,0:T(8,128)(2,1)} reshape(bf16[64,64,2,128]{3,2,1,0:T(2,128)(2,1)} %copy.167) | data formatting | bytes 4194304 | tf_op jit(solution)/shard_map/reshape;reshape | solution.py:185
  160.0 7.5 %all-to-all-start.2 = ((bf16[32,2,64,256]{3,2,1,0:T(8,128)(2,1)}), bf16[32,2,64,256]{3,2,1,0:T(8,128)(2,1)}, u32[]{:S(2)}, u32[]{:S(2)}) async-start(bf16[32,2,64,256]{3,2,1,0:T(8,128)(2,1)} %reshape_reshape.8), calls=%async_computation.2 | async-start | bytes 4194304 | tf_op jit(solution)/shard_map/all_to_all | solution.py:184
  168.6 2.9 %fusion.25 = bf16[256,256]{1,0:T(8,128)(2,1)S(1)} fusion(bf16[4096,256]{1,0:T(8,128)(2,1)} %param.14, bf16[256,8192]{1,0:T(8,128)(2,1)} %copy-done.4, s32[]{:T(128)S(6)} %select_n.186), kind=kOutput, calls=%fused_computation.43 | convolution fusion | flops 536936448 | bytes 4325380 | tf_op jit(solution)/shard_map/dot_general | solution.py:138
  173.3 1.0 copy.165
  174.5 19.0 %all-to-all-done.2 = bf16[32,2,64,256]{3,2,1,0:T(8,128)(2,1)} async-done(((bf16[32,2,64,256]{3,2,1,0:T(8,128)(2,1)}), bf16[32,2,64,256]{3,2,1,0:T(8,128)(2,1)}, u32[]{:S(2)}, u32[]{:S(2)}) %all-to-all-start.2) | async-done | bytes 2097184 | tf_op jit(solution)/shard_map/all_to_all | solution.py:184
  193.4 3.0 %gather_fusion.10 = bf16[12,64,256]{2,1,0:T(8,128)(2,1)} fusion(bf16[32,2,64,256]{3,2,1,0:T(8,128)(2,1)} %all-to-all-done.2, s32[12]{0:T(128)S(1)} %get-tuple-element.20), kind=kCustom, calls=%fused_computation.10 | custom fusion | bytes 786528 | tf_op jit(solution)/shard_map/gather | solution.py:198
  196.4 1.4 reshape.496
  197.8 2.4 fusion.32
  200.5 2.1 convolution_convert_fusion
  202.6 41.3 %reduce-scatter.2.cloned.1.call-done = bf16[256,512]{1,0:T(8,128)(2,1)} async-done(((bf16[256,4096]{1,0:T(8,128)(2,1)}), bf16[256,512]{1,0:T(8,128)(2,1)}) %reduce-scatter.2.cloned.1.call-update) | async-done | bytes 262160 | tf_op jit(solution)/shard_map/reduce_scatter | solution.py:210
  243.9 1.1 fusion.36
  245.0 15.2 %psum.7 = f32[256]{0:T(256)S(1)} all-reduce(f32[256]{0:T(256)S(1)} %fusion.36), channel_id=1, replica_groups=mesh['leaf'=32,'mp'=8] {'mp'}, use_global_device_ids=true, to_apply=%region_12.13 | all-reduce | flops 256 | bytes 2048 | tf_op jit(solution)/shard_map/psum | solution.py:213
  260.1 1.8 fusion.35
  (121 shorter events, 13.2 us)
Async XLA Ops:
  6.5 193.9 %copy-start = (bf16[256,4096]{1,0:T(8,128)(2,1)S(1)}, bf16[256,4096]{1,0:T(8,128)(2,1)}, u32[]{:S(2)}) copy-start(bf16[256,4096]{1,0:T(8,128)(2,1)} %param.15) | copy-start | bytes 6291460
  6.5 41.7 %collective-permute-start = (bf16[256,512]{1,0:T(8,128)(2,1)}, bf16[256,512]{1,0:T(8,128)(2,1)S(1)}, u32[]{:S(2)}, u32[]{:S(2)}) collective-permute-start(bf16[256,512]{1,0:T(8,128)(2,1)} %param.11), channel_id=1, source_target_pairs={{0,1},{1,2},{2,3},{3,4},{4,5},{5,6},{6,7},{7,0},{8,9},{9,10},{10,1... | collective-permute-start | bytes 786440 | tf_op jit(solution)/shard_map/ppermute | solution.py:28
  8.5 49.1 %collective-permute-start.4 = (bf16[256,512]{1,0:T(8,128)(2,1)}, bf16[256,512]{1,0:T(8,128)(2,1)S(1)}, u32[]{:S(2)}, u32[]{:S(2)}) collective-permute-start(bf16[256,512]{1,0:T(8,128)(2,1)} %param.11), channel_id=1, source_target_pairs={{0,7},{1,0},{2,1},{3,2},{4,3},{5,4},{6,5},{7,6},{8,15},{9,8},{10,9... | collective-permute-start | bytes 786440 | tf_op jit(solution)/shard_map/ppermute | solution.py:31
  21.5 25.5 %copy-start.1 = (s32[256]{0:T(256)S(1)}, s32[256]{0:T(256)}, u32[]{:S(2)}) copy-start(s32[256]{0:T(256)} %param.20) | copy-start | bytes 3076
  21.5 54.0 %copy-start.5 = (bf16[256,512]{1,0:T(8,128)(2,1)S(1)}, bf16[256,512]{1,0:T(8,128)(2,1)}, u32[]{:S(2)}) copy-start(bf16[256,512]{1,0:T(8,128)(2,1)} %param.11) | copy-start | bytes 786436
  48.3 9.1 %collective-permute-start.1 = (bf16[256,512]{1,0:T(8,128)(2,1)S(1)}, bf16[256,512]{1,0:T(8,128)(2,1)S(1)}, u32[]{:S(2)}, u32[]{:S(2)}) collective-permute-start(bf16[256,512]{1,0:T(8,128)(2,1)S(1)} %collective-permute-done), channel_id=1, source_target_pairs={{0,1},{1,2},{2,3},{3,4},{4,5},{5,6},{6,7},{7,0},{8,9},{9,10},{10,1... | collective-permute-start | bytes 786440 | tf_op jit(solution)/shard_map/ppermute | solution.py:28
  57.3 8.2 %collective-permute-start.2 = (bf16[256,512]{1,0:T(8,128)(2,1)S(1)}, bf16[256,512]{1,0:T(8,128)(2,1)}, u32[]{:S(2)}, u32[]{:S(2)}) collective-permute-start(bf16[256,512]{1,0:T(8,128)(2,1)S(1)} %collective-permute-done.1), channel_id=1, source_target_pairs={{0,1},{1,2},{2,3},{3,4},{4,5},{5,6},{6,7},{7,0},{8,9},{9,10},{10,1... | collective-permute-start | bytes 786440 | tf_op jit(solution)/shard_map/ppermute | solution.py:28
  57.5 8.5 %collective-permute-start.5 = (bf16[256,512]{1,0:T(8,128)(2,1)S(1)}, bf16[256,512]{1,0:T(8,128)(2,1)}, u32[]{:S(2)}, u32[]{:S(2)}) collective-permute-start(bf16[256,512]{1,0:T(8,128)(2,1)S(1)} %collective-permute-done.4), channel_id=1, source_target_pairs={{0,7},{1,0},{2,1},{3,2},{4,3},{5,4},{6,5},{7,6},{8,15},{9,8},{10,9... | collective-permute-start | bytes 786440 | tf_op jit(solution)/shard_map/ppermute | solution.py:31
  65.6 7.9 %collective-permute-start.3 = (bf16[256,512]{1,0:T(8,128)(2,1)}, bf16[256,512]{1,0:T(8,128)(2,1)}, u32[]{:S(2)}, u32[]{:S(2)}) collective-permute-start(bf16[256,512]{1,0:T(8,128)(2,1)} %collective-permute-done.2), channel_id=1, source_target_pairs={{0,1},{1,2},{2,3},{3,4},{4,5},{5,6},{6,7},{7,0},{8,9},{9,10},{10,1... | collective-permute-start | bytes 786440 | tf_op jit(solution)/shard_map/ppermute | solution.py:28
  66.0 13.9 %copy-start.6 = (bf16[4096,256]{1,0:T(8,128)(2,1)S(1)}, bf16[4096,256]{1,0:T(8,128)(2,1)}, u32[]{:S(2)}) copy-start(bf16[4096,256]{1,0:T(8,128)(2,1)} %param.13) | copy-start | bytes 6291460
  66.0 10.5 %collective-permute-start.6 = (bf16[256,512]{1,0:T(8,128)(2,1)}, bf16[256,512]{1,0:T(8,128)(2,1)S(1)}, u32[]{:S(2)}, u32[]{:S(2)}) collective-permute-start(bf16[256,512]{1,0:T(8,128)(2,1)} %collective-permute-done.5), channel_id=1, source_target_pairs={{0,7},{1,0},{2,1},{3,2},{4,3},{5,4},{6,5},{7,6},{8,15},{9,8},{10,9... | collective-permute-start | bytes 786440 | tf_op jit(solution)/shard_map/ppermute | solution.py:31
  77.6 3.3 %copy-start.7 = (bf16[4096,256]{1,0:T(8,128)(2,1)S(1)}, bf16[4096,256]{1,0:T(8,128)(2,1)}, u32[]{:S(2)}) copy-start(bf16[4096,256]{1,0:T(8,128)(2,1)} %param.12) | copy-start | bytes 6291460
  79.9 2.0 copy-start.4
  84.1 17.1 %copy-start.2 = (bf16[8,256,256]{2,1,0:T(8,128)(2,1)S(1)}, bf16[8,256,256]{2,1,0:T(8,128)(2,1)}, u32[]{:S(2)}) copy-start(bf16[8,256,256]{2,1,0:T(8,128)(2,1)} %param.17) | copy-start | bytes 3145732
  88.6 33.6 %all-to-all-start = ((bf16[32,2,64,256]{3,2,1,0:T(8,128)(2,1)}), bf16[32,2,64,256]{3,2,1,0:T(8,128)(2,1)}, u32[]{:S(2)}, u32[]{:S(2)}) async-start(bf16[32,2,64,256]{3,2,1,0:T(8,128)(2,1)} %scatter_fusion), calls=%async_computation | async-start | bytes 4194304 | tf_op jit(solution)/shard_map/all_to_all | solution.py:172
  106.5 6.5 %copy-start.11 = (pred[64]{0:T(512)(128)(4,1)S(1)}, pred[64]{0:T(512)(128)(4,1)}, u32[]{:S(2)}) copy-start(pred[64]{0:T(512)(128)(4,1)} %ge.35) | copy-start | bytes 196
  133.4 3.6 %copy-start.3 = (f32[64,2,64,256]{3,2,1,0:T(8,128)}, f32[64,2,64,256]{3,2,1,0:T(8,128)S(1)}, u32[]{:S(2)}) copy-start(f32[64,2,64,256]{3,2,1,0:T(8,128)S(1)} %get-tuple-element.25) | copy-start | bytes 25165828
  137.7 22.2 %all-to-all-start.1 = ((bf16[32,2,128]{2,1,0:T(2,128)(2,1)}), bf16[32,2,128]{2,1,0:T(2,128)(2,1)S(1)}, u32[]{:S(2)}, u32[]{:S(2)}) async-start(bf16[32,2,128]{2,1,0:T(2,128)(2,1)} %reshape.599), calls=%async_computation.1 | async-start | bytes 32768 | tf_op jit(solution)/shard_map/all_to_all | solution.py:191
  155.5 12.2 %copy-start.9 = (bf16[256,2,64]{0,2,1:T(8,128)(2,1)S(1)}, bf16[256,2,64]{0,2,1:T(8,128)(2,1)}, u32[]{:S(2)}) copy-start(bf16[256,2,64]{0,2,1:T(8,128)(2,1)} %get-tuple-element.10) | copy-start | bytes 196612
  155.5 12.5 %copy-start.8 = (bf16[256,2,64]{0,2,1:T(8,128)(2,1)S(1)}, bf16[256,2,64]{0,2,1:T(8,128)(2,1)}, u32[]{:S(2)}) copy-start(bf16[256,2,64]{0,2,1:T(8,128)(2,1)} %get-tuple-element.9) | copy-start | bytes 196612
  160.0 33.4 %all-to-all-start.2 = ((bf16[32,2,64,256]{3,2,1,0:T(8,128)(2,1)}), bf16[32,2,64,256]{3,2,1,0:T(8,128)(2,1)}, u32[]{:S(2)}, u32[]{:S(2)}) async-start(bf16[32,2,64,256]{3,2,1,0:T(8,128)(2,1)} %reshape_reshape.8), calls=%async_computation.2 | async-start | bytes 4194304 | tf_op jit(solution)/shard_map/all_to_all | solution.py:184
  167.4 76.4 %reduce-scatter.2.cloned.1.call-start = ((), (), s32[]{:S(2)}) async-start(), calls=%async_computation.4 | async-start | bytes 2359296 | tf_op jit(solution)/shard_map/reduce_scatter | solution.py:210
  197.7 62.4 %copy-start.10 = (f32[512]{0:T(512)S(1)}, f32[512]{0:T(512)}, u32[]{:S(2)}) copy-start(f32[512]{0:T(512)} %param.16) | copy-start | bytes 6148
Sparse Core Ops, SparseCore 0:
  202.7 41.1 reduce-scatter.1
